TPU v7x, 128 devices: a whole 4x4x4 slice. The times are simulated.
128 devices in a mesh: row: 8 (over x, y_hi), col: 16 (over z, y_lo, core).
Axes of the slice: x: 4, y: 4 (y_hi: 2, y_lo: 2; y = y_hi * 2 + y_lo), z: 4, core: 2. Of those that a mesh axis runs over, the one named last changes fastest.
Arguments:
- normal_slab: float32 [8192, 16384], P('row', 'col'), may hold values from -6 to 6
- left_design: float32 [3, 1024, 8192], P(None, 'col', 'row'), may hold values from -1.2 to 1.2
- right_design: float32 [3, 1024, 16384], P(None, 'row', 'col'), may hold values from -1.2 to 1.2
- estimate: float32 [16384], P('col'), may hold values from -0.25 to 0.25
- observed: float32 [3, 1024], P(None, 'row'), may hold values from -6 to 6
- arc_id: int32 [3, 1024], P(None, 'row'), may hold values from 0 to 63
- arc_bias: float32 [64], replicated, may hold values from -5 to 5
Outputs:
- updated_slab: float32 [8192, 16384], P('row', 'col')
All inputs are finite; a program needn't handle non-finite values.
Results may differ from a plain program's by a relative error of at most 0.0001.
Values sent between devices are 32-bit elements; how exact they have to be, the bound alone decides.
A program may use at most 128 MiB of HBM per device.

v0:
```python
import jax
import jax.numpy as jnp
from jax import lax
from jax.sharding import PartitionSpec as P


def gathered_total(x, axis):
    tiles = lax.all_gather(x, axis)
    return tiles.sum(axis=0)


def contract(left_rows, right_rows, weights):
    return lax.dot_general(
        left_rows * weights[:, None],
        right_rows,
        (((0,), (0,)), ((), ())),
        precision=lax.Precision.HIGHEST,
    )


def local(normal_slab, left_design, right_design, estimate, observed, arc_id, arc_bias):
    highest = lax.Precision.HIGHEST
    one_hot = arc_id[:, :, None] == jnp.arange(arc_bias.shape[0], dtype=jnp.int32)[None, None, :]
    arc_offset = jnp.sum(jnp.where(one_hot, arc_bias[None, None, :], jnp.float32(0.0)), axis=2)
    running = normal_slab
    for number in range(right_design.shape[0]):
        partial_sum = jnp.dot(right_design[number], estimate, precision=highest)
        summed = gathered_total(partial_sum, "col")
        residual = observed[number] - summed - arc_offset[number]
        weights = 1.0 / (1.0 + residual * residual)
        left_all = lax.all_gather(left_design[number], "col", axis=0, tiled=True)
        right_rows = lax.all_gather(right_design[number], "row", axis=0, tiled=True)
        weight_rows = lax.all_gather(weights, "row", axis=0, tiled=True)
        running = running + contract(left_all, right_rows, weight_rows)
    return running


def solution(mesh):
    in_specs = (
        P("row", "col"),
        P(None, "col", "row"),
        P(None, "row", "col"),
        P("col"),
        P(None, "row"),
        P(None, "row"),
        P(),
    )
    out_specs = P("row", "col")
    return jax.shard_map(local, mesh=mesh, in_specs=in_specs, out_specs=out_specs, check_vma=False)
```

profile of v0, /device:TPU:1, one launch (start us, length us, event | category | flops | bytes accessed | tf_op | source)
XLA Modules:
  0.0 382.7 jit_solution(7969491137729842434)
XLA Ops:
  6.6 0.0 all-gather.32.cloned.1.call-start
  6.6 2.7 fusion.23
  9.3 0.0 all-gather.32.cloned.1.call-update
  9.4 0.0 all-gather.30.cloned.1.call-start
  9.4 0.9 fusion.24
  10.4 0.0 all-gather.30.cloned.1.call-update
  10.4 0.0 all-gather.28.cloned.1.call-start
  10.4 0.7 all-gather.28.cloned.1.call-update
  11.1 0.0 all-gather.26.cloned.1.call-start
  11.2 0.5 all-gather.26.cloned.1.call-update
  11.7 0.0 all-gather.24.cloned.1.call-start
  11.7 0.5 all-gather.24.cloned.1.call-update
  12.3 0.0 all-gather.22.cloned.1.call-start
  12.3 0.5 all-gather.22.cloned.1.call-update
  12.9 0.5 convolution_bitcast_fusion.2
  13.4 22.2 %all-gather.9 = f32[16,1,128]{2,1,0:T(1,128)S(1)} all-gather(f32[1,1,128]{2,1,0:T(1,128)S(1)} %convolution_bitcast_fusion.2), channel_id=3, replica_groups=mesh['row'=8,'col'=16] {'col'}, dimensions={0}, use_global_device_ids=true | all-gather | bytes 8704 | tf_op jit(solution)/shard_map/all_gather | solution.py:8
  35.6 0.5 convolution_bitcast_fusion.1
  36.1 16.1 %all-gather.11 = f32[16,1,128]{2,1,0:T(1,128)S(1)} all-gather(f32[1,1,128]{2,1,0:T(1,128)S(1)} %convolution_bitcast_fusion.1), channel_id=6, replica_groups=mesh['row'=8,'col'=16] {'col'}, dimensions={0}, use_global_device_ids=true | all-gather | bytes 8704 | tf_op jit(solution)/shard_map/all_gather | solution.py:8
  52.3 0.5 convolution_bitcast_fusion
  52.8 17.6 %all-gather.13 = f32[16,1,128]{2,1,0:T(1,128)S(1)} all-gather(f32[1,1,128]{2,1,0:T(1,128)S(1)} %convolution_bitcast_fusion), channel_id=9, replica_groups=mesh['row'=8,'col'=16] {'col'}, dimensions={0}, use_global_device_ids=true | all-gather | bytes 8704 | tf_op jit(solution)/shard_map/all_gather | solution.py:8
  70.4 0.1 select_reduce_fusion
  70.5 19.3 %all-gather.14 = f32[8,1,128]{2,1,0:T(1,128)S(1)} all-gather(f32[1,1,128]{2,1,0:T(1,128)S(1)} %get-tuple-element.12), channel_id=1, replica_groups=mesh['row'=8,'col'=16] {'row'}, dimensions={0}, use_global_device_ids=true | all-gather | bytes 4608 | tf_op jit(solution)/shard_map/all_gather | solution.py:33
  89.8 14.5 %all-gather.12 = f32[8,1,128]{2,1,0:T(1,128)S(1)} all-gather(f32[1,1,128]{2,1,0:T(1,128)S(1)} %get-tuple-element.13), channel_id=1, replica_groups=mesh['row'=8,'col'=16] {'row'}, dimensions={0}, use_global_device_ids=true | all-gather | bytes 4608 | tf_op jit(solution)/shard_map/all_gather | solution.py:33
  104.3 17.5 %all-gather.10 = f32[8,1,128]{2,1,0:T(1,128)S(1)} all-gather(f32[1,1,128]{2,1,0:T(1,128)S(1)} %get-tuple-element.11), channel_id=1, replica_groups=mesh['row'=8,'col'=16] {'row'}, dimensions={0}, use_global_device_ids=true | all-gather | bytes 4608 | tf_op jit(solution)/shard_map/all_gather | solution.py:33
  121.9 0.3 all-gather.30.cloned.1.call-done
  122.2 18.2 %fusion = f32[1024,1024]{1,0:T(8,128)} fusion(f32[1,1024,1024]{2,1,0:T(8,128)} %all-gather.32.cloned.1.call-done, f32[1,1024,1024]{2,1,0:T(8,128)} %all-gather.30.cloned.1.call-done, f32[1024]{0:T(1024)S(1)} %bitcast.105), kind=kOutput, calls=%fused_computation | convolution fusion | flops 12885950464 | bytes 12587008 | tf_op jit(solution)/shard_map/dot_general | solution.py:13
  140.4 54.8 %all-gather.28.cloned.1.call-done = f32[1,1024,1024]{2,1,0:T(8,128)} async-done(((f32[1,128,1024]{2,1,0:T(8,128)}), f32[1,1024,1024]{2,1,0:T(8,128)}) %all-gather.28.cloned.1.call-update) | async-done | bytes 4194320 | tf_op jit(solution)/shard_map/all_gather | solution.py:32
  195.2 37.8 %all-gather.26.cloned.1.call-done = f32[1,1024,1024]{2,1,0:T(8,128)} async-done(((f32[1,64,1024]{2,1,0:T(8,128)}), f32[1,1024,1024]{2,1,0:T(8,128)}) %all-gather.26.cloned.1.call-update) | async-done | bytes 4194320 | tf_op jit(solution)/shard_map/all_gather | solution.py:31
  232.9 18.3 %fusion.2 = f32[1024,1024]{1,0:T(8,128)} fusion(f32[1,1024,1024]{2,1,0:T(8,128)} %all-gather.28.cloned.1.call-done, f32[1,1024,1024]{2,1,0:T(8,128)} %all-gather.26.cloned.1.call-done, f32[1024]{0:T(1024)S(1)} %bitcast.104), kind=kOutput, calls=%fused_computation.3 | convolution fusion | flops 12885950464 | bytes 12587008 | tf_op jit(solution)/shard_map/dot_general | solution.py:13
  251.2 54.6 %all-gather.24.cloned.1.call-done = f32[1,1024,1024]{2,1,0:T(8,128)} async-done(((f32[1,128,1024]{2,1,0:T(8,128)}), f32[1,1024,1024]{2,1,0:T(8,128)}) %all-gather.24.cloned.1.call-update) | async-done | bytes 4194320 | tf_op jit(solution)/shard_map/all_gather | solution.py:32
  305.8 37.8 %all-gather.22.cloned.1.call-done = f32[1,1024,1024]{2,1,0:T(8,128)} async-done(((f32[1,64,1024]{2,1,0:T(8,128)}), f32[1,1024,1024]{2,1,0:T(8,128)}) %all-gather.22.cloned.1.call-update) | async-done | bytes 4194320 | tf_op jit(solution)/shard_map/all_gather | solution.py:31
  343.6 32.2 %add_add_fusion = f32[1024,1024]{1,0:T(8,128)} fusion(f32[1024,1024]{1,0:T(8,128)} %fusion, f32[1024,1024]{1,0:T(8,128)} %fusion.2, f32[1024,1024]{1,0:T(8,128)} %param.7, f32[1,1024,1024]{2,1,0:T(8,128)} %all-gather.24.cloned.1.call-done, f32[1,1024,1024]{2,1,0:T(8,128)} %all-gather.22.cloned.1.call-done, f32[1024]{0:T(1024)S(1)} %bitcast.103), kind=kOutput, calls=%fused_computation.9 | convolution fusion | flops 12889096192 | bytes 25169920 | tf_op jit(solution)/shard_map/dot_general | solution.py:13
  (17 shorter events, 0.1 us)
Async XLA Ops:
  6.5 6.3 %copy-start = (f32[1024]{0:T(1024)S(1)}, f32[1024]{0:T(1024)}, u32[]{:S(2)}) copy-start(f32[1024]{0:T(1024)} %param.10) | copy-start | bytes 12292
  6.5 6.3 %copy-start.1 = (f32[3,128,1024]{2,1,0:T(8,128)S(1)}, f32[3,128,1024]{2,1,0:T(8,128)}, u32[]{:S(2)}) copy-start(f32[3,128,1024]{2,1,0:T(8,128)} %param.9) | copy-start | bytes 4718596
  6.5 2.9 copy-start.2
  6.5 63.8 %copy-start.3 = (s32[3,128]{1,0:T(4,128)S(1)}, s32[3,128]{1,0:T(4,128)}, u32[]{:S(2)}) copy-start(s32[3,128]{1,0:T(4,128)} %param.12) | copy-start | bytes 4612
  6.5 63.8 %copy-start.5 = (f32[64]{0:T(128)S(1)}, f32[64]{0:T(128)}, u32[]{:S(2)}) copy-start(f32[64]{0:T(128)} %param.13) | copy-start | bytes 772
  6.5 63.9 %copy-start.4 = (f32[3,128]{1,0:T(4,128)S(1)}, f32[3,128]{1,0:T(4,128)}, u32[]{:S(2)}) copy-start(f32[3,128]{1,0:T(4,128)} %param.11) | copy-start | bytes 4612
  6.6 115.3 %all-gather.32.cloned.1.call-start = ((), (), s32[]{:S(2)}) async-start(), calls=%async_computation.5 | async-start | bytes 4718592 | tf_op jit(solution)/shard_map/all_gather | solution.py:32
  9.4 112.8 %all-gather.30.cloned.1.call-start = ((), (), s32[]{:S(2)}) async-start(), calls=%async_computation.4 | async-start | bytes 4456448 | tf_op jit(solution)/shard_map/all_gather | solution.py:31
  10.4 184.8 %all-gather.28.cloned.1.call-start = ((), (), s32[]{:S(2)}) async-start(), calls=%async_computation.3 | async-start | bytes 4718592 | tf_op jit(solution)/shard_map/all_gather | solution.py:32
  11.1 221.8 %all-gather.26.cloned.1.call-start = ((), (), s32[]{:S(2)}) async-start(), calls=%async_computation.2 | async-start | bytes 4456448 | tf_op jit(solution)/shard_map/all_gather | solution.py:31
  11.7 294.1 %all-gather.24.cloned.1.call-start = ((), (), s32[]{:S(2)}) async-start(), calls=%async_computation.1 | async-start | bytes 4718592 | tf_op jit(solution)/shard_map/all_gather | solution.py:32
  12.3 331.3 %all-gather.22.cloned.1.call-start = ((), (), s32[]{:S(2)}) async-start(), calls=%async_computation | async-start | bytes 4456448 | tf_op jit(solution)/shard_map/all_gather | solution.py:31
Sparse Core Ops, SparseCore 0:
  9.7 74.3 all-gather.31
  85.9 36.2 all-gather.29
  124.5 70.5 all-gather.27
  196.7 36.1 all-gather.25
  235.1 70.6 all-gather.23
  307.4 36.1 all-gather.21
where the time goes:
time: 383 us
  waiting for transfers between devices  188 us (49%)
  blocking collectives  107 us (28%)
  matrix products  70.3 us (18%)
  between operations  13.5 us (4%)
    all_gather x3, waiting for transfers between devices, local(): right_rows = lax.all_gather(right_design[number], 'row', axis=0, tiled=True)  109 us
    all_gather x3, waiting for transfers between devices, local(): left_all = lax.all_gather(left_design[number], 'col', axis=0, tiled=True)  75.9 us
    dot_general x3, matrix products, contract(): lax.dot_general(left_rows * weights[:, None], right_rows, (((0,), (0,)),...  68.7 us
    all_gather x3, blocking collectives, gathered_total(): tiles = lax.all_gather(x, axis)  55.8 us
    all_gather x3, blocking collectives, local(): weight_rows = lax.all_gather(weights, 'row', axis=0, tiled=True)  51.4 us
  transfers between devices with their start and end apart: 6, of which 5 were waited for; matrix products, arithmetic and copies ran while one was open for 10% of the time, Pallas kernels for 0%

commit v1 on v0

--- a/solution.py
+++ b/solution.py
@@ -28,7 +28,11 @@
         summed = gathered_total(partial_sum, "col")
         residual = observed[number] - summed - arc_offset[number]
         weights = 1.0 / (1.0 + residual * residual)
-        left_all = lax.all_gather(left_design[number], "col", axis=0, tiled=True)
+        own = left_design[number]
+        size = lax.axis_size("col")
+        pieces = jnp.stack([own for _ in range(size)])
+        pieces = lax.all_to_all(pieces, "col", split_axis=0, concat_axis=0)
+        left_all = jnp.concatenate(pieces, axis=0)
         right_rows = lax.all_gather(right_design[number], "row", axis=0, tiled=True)
         weight_rows = lax.all_gather(weights, "row", axis=0, tiled=True)
         running = running + contract(left_all, right_rows, weight_rows)

time: 383 us -> 423 us (1.10)
  the two profiles are of different devices: /device:TPU:1 before, /device:TPU:0 now
where the time goes in v1:
time: 423 us; the launch traced here: 422 us
  blocking collectives  249 us (59%)
  matrix products  68.5 us (16%)
  waiting for transfers between devices  60.3 us (14%)
  other arithmetic  13.7 us (3%)
  between operations  13.2 us (3%)
  starting transfers between devices  9.32 us (2%)
  local copies, waits for them, and re-layouts  8.33 us (2%)
    all_gather x3, blocking collectives, gathered_total(): tiles = lax.all_gather(x, axis)  106 us
    all_to_all x1, blocking collectives, local(): pieces = lax.all_to_all(pieces, 'col', split_axis=0, concat_axis=0)  79.7 us
    dot_general x3, matrix products, contract(): lax.dot_general(left_rows * weights[:, None], right_rows, (((0,), (0,)),...  67 us
    all_gather x3, blocking collectives, local(): weight_rows = lax.all_gather(weights, 'row', axis=0, tiled=True)  62.7 us
    all_to_all x2, waiting for transfers between devices, local(): pieces = lax.all_to_all(pieces, 'col', split_axis=0, concat_axis=0)  58.9 us
    mul x3, other arithmetic, contract(): left_rows * weights[:, None]  13.5 us
    all_to_all x2, starting transfers between devices, local(): pieces = lax.all_to_all(pieces, 'col', split_axis=0, concat_axis=0)  9.24 us
  transfers between devices with their start and end apart: 5, of which 1 were waited for; matrix products, arithmetic and copies ran while one was open for 13% of the time, Pallas kernels for 0%

profile of v1, /device:TPU:0, one launch (start us, length us, event | category | flops | bytes accessed | tf_op | source)
XLA Modules:
  0.0 422.1 jit_solution(4852006620274418061)
XLA Ops:
  6.5 0.0 all-gather.20.cloned.1.call-start
  6.5 2.7 fusion.20
  9.2 0.0 all-gather.20.cloned.1.call-update
  9.3 0.0 all-gather.18.cloned.1.call-start
  9.3 0.7 all-gather.18.cloned.1.call-update
  10.0 0.1 slice_bitcast_fusion.2
  10.1 0.5 stack.11
  10.6 79.7 %all_to_all.15 = f32[16,64,1024]{2,1,0:T(8,128)} all-to-all(f32[16,64,1024]{2,1,0:T(8,128)S(1)} %stack.11), channel_id=1, replica_groups=mesh['row'=8,'col'=16] {'col'}, dimensions={0} | all-to-all | bytes 8388608 | tf_op jit(solution)/shard_map/all_to_all | solution.py:34
  90.3 2.5 stack.10
  92.9 4.6 %all-to-all-start.1 = ((f32[16,64,1024]{2,1,0:T(8,128)}), f32[16,64,1024]{2,1,0:T(8,128)}, u32[]{:S(2)}, u32[]{:S(2)}) async-start(f32[16,64,1024]{2,1,0:T(8,128)} %stack.10), calls=%async_computation.1 | async-start | bytes 8388608 | tf_op jit(solution)/shard_map/all_to_all | solution.py:34
  97.4 0.0 all-gather.16.cloned.1.call-start
  97.5 0.7 all-gather.16.cloned.1.call-update
  98.2 58.9 %all-to-all-done.1 = f32[16,64,1024]{2,1,0:T(8,128)} async-done(((f32[16,64,1024]{2,1,0:T(8,128)}), f32[16,64,1024]{2,1,0:T(8,128)}, u32[]{:S(2)}, u32[]{:S(2)}) %all-to-all-start.1) | async-done | bytes 4194336 | tf_op jit(solution)/shard_map/all_to_all | solution.py:34
  157.1 2.5 stack.9
  159.6 4.7 %all-to-all-start = ((f32[16,64,1024]{2,1,0:T(8,128)}), f32[16,64,1024]{2,1,0:T(8,128)}, u32[]{:S(2)}, u32[]{:S(2)}) async-start(f32[16,64,1024]{2,1,0:T(8,128)} %stack.9), calls=%async_computation | async-start | bytes 8388608 | tf_op jit(solution)/shard_map/all_to_all | solution.py:34
  164.3 0.5 convolution_bitcast_fusion.2
  164.8 72.6 %all-gather.6 = f32[16,1,128]{2,1,0:T(1,128)S(1)} all-gather(f32[1,1,128]{2,1,0:T(1,128)S(1)} %convolution_bitcast_fusion.2), channel_id=2, replica_groups=mesh['row'=8,'col'=16] {'col'}, dimensions={0}, use_global_device_ids=true | all-gather | bytes 8704 | tf_op jit(solution)/shard_map/all_gather | solution.py:8
  237.5 0.5 convolution_bitcast_fusion.1
  238.0 17.4 %all-gather.8 = f32[16,1,128]{2,1,0:T(1,128)S(1)} all-gather(f32[1,1,128]{2,1,0:T(1,128)S(1)} %convolution_bitcast_fusion.1), channel_id=4, replica_groups=mesh['row'=8,'col'=16] {'col'}, dimensions={0}, use_global_device_ids=true | all-gather | bytes 8704 | tf_op jit(solution)/shard_map/all_gather | solution.py:8
  255.4 0.5 convolution_bitcast_fusion
  255.9 16.3 %all-gather.10 = f32[16,1,128]{2,1,0:T(1,128)S(1)} all-gather(f32[1,1,128]{2,1,0:T(1,128)S(1)} %convolution_bitcast_fusion), channel_id=6, replica_groups=mesh['row'=8,'col'=16] {'col'}, dimensions={0}, use_global_device_ids=true | all-gather | bytes 8704 | tf_op jit(solution)/shard_map/all_gather | solution.py:8
  272.3 0.1 select_reduce_fusion
  272.4 23.2 %all-gather.11 = f32[8,1,128]{2,1,0:T(1,128)S(1)} all-gather(f32[1,1,128]{2,1,0:T(1,128)S(1)} %get-tuple-element.12), channel_id=1, replica_groups=mesh['row'=8,'col'=16] {'row'}, dimensions={0}, use_global_device_ids=true | all-gather | bytes 4608 | tf_op jit(solution)/shard_map/all_gather | solution.py:37
  295.6 18.0 %all-gather.9 = f32[8,1,128]{2,1,0:T(1,128)S(1)} all-gather(f32[1,1,128]{2,1,0:T(1,128)S(1)} %get-tuple-element.13), channel_id=1, replica_groups=mesh['row'=8,'col'=16] {'row'}, dimensions={0}, use_global_device_ids=true | all-gather | bytes 4608 | tf_op jit(solution)/shard_map/all_gather | solution.py:37
  313.6 21.5 %all-gather.7 = f32[8,1,128]{2,1,0:T(1,128)S(1)} all-gather(f32[1,1,128]{2,1,0:T(1,128)S(1)} %get-tuple-element.11), channel_id=1, replica_groups=mesh['row'=8,'col'=16] {'row'}, dimensions={0}, use_global_device_ids=true | all-gather | bytes 4608 | tf_op jit(solution)/shard_map/all_gather | solution.py:37
  335.1 4.5 %bitcast_multiply_fusion = f32[1024,1024]{1,0:T(8,128)} fusion(f32[16,64,1024]{2,1,0:T(8,128)} %all_to_all.15, f32[1024]{0:T(1024)S(1)} %bitcast.109), kind=kLoop, calls=%fused_computation.2 | loop fusion | flops 1048576 | bytes 8392704 | tf_op jit(solution)/shard_map/mul | solution.py:14
  339.6 4.5 %bitcast_multiply_fusion.1 = f32[1024,1024]{1,0:T(8,128)} fusion(f32[16,64,1024]{2,1,0:T(8,128)} %all-to-all-done.1, f32[1024]{0:T(1024)S(1)} %bitcast.108), kind=kLoop, calls=%fused_computation.5 | loop fusion | flops 1048576 | bytes 8392704 | tf_op jit(solution)/shard_map/mul | solution.py:14
  344.1 0.0 all-to-all-done
  344.1 4.5 %bitcast_multiply_fusion.2 = f32[1024,1024]{1,0:T(8,128)} fusion(f32[16,64,1024]{2,1,0:T(8,128)} %all-to-all-done, f32[1024]{0:T(1024)S(1)} %bitcast.107), kind=kLoop, calls=%fused_computation.8 | loop fusion | flops 1048576 | bytes 8392704 | tf_op jit(solution)/shard_map/mul | solution.py:14
  348.6 17.6 %fusion = f32[1024,1024]{1,0:T(8,128)} fusion(f32[1024,1024]{1,0:T(8,128)} %bitcast_multiply_fusion, f32[1,1024,1024]{2,1,0:T(8,128)} %all-gather.20.cloned.1.call-done), kind=kOutput, calls=%fused_computation | convolution fusion | flops 12884901888 | bytes 12582912 | tf_op jit(solution)/shard_map/dot_general | solution.py:13
  366.2 17.6 %fusion.2 = f32[1024,1024]{1,0:T(8,128)} fusion(f32[1024,1024]{1,0:T(8,128)} %bitcast_multiply_fusion.1, f32[1,1024,1024]{2,1,0:T(8,128)} %all-gather.18.cloned.1.call-done), kind=kOutput, calls=%fused_computation.3 | convolution fusion | flops 12884901888 | bytes 12582912 | tf_op jit(solution)/shard_map/dot_general | solution.py:13
  383.7 31.8 %add_add_fusion = f32[1024,1024]{1,0:T(8,128)} fusion(f32[1024,1024]{1,0:T(8,128)} %fusion, f32[1024,1024]{1,0:T(8,128)} %fusion.2, f32[1024,1024]{1,0:T(8,128)} %param.7, f32[1024,1024]{1,0:T(8,128)} %bitcast_multiply_fusion.2, f32[1,1024,1024]{2,1,0:T(8,128)} %all-gather.16.cloned.1.call-done), kind=kOutput, calls=%fused_computation.9 | convolution fusion | flops 12888047616 | bytes 25165824 | tf_op jit(solution)/shard_map/dot_general | solution.py:13
  (21 shorter events, 0.1 us)
Async XLA Ops:
  6.5 157.8 %copy-start = (f32[1024]{0:T(1024)S(1)}, f32[1024]{0:T(1024)}, u32[]{:S(2)}) copy-start(f32[1024]{0:T(1024)} %param.10) | copy-start | bytes 12292
  6.5 3.5 copy-start.3
  6.5 342.0 %all-gather.20.cloned.1.call-start = ((), (), s32[]{:S(2)}) async-start(), calls=%async_computation.5 | async-start | bytes 4718592 | tf_op jit(solution)/shard_map/all_gather | solution.py:36
  9.3 356.9 %all-gather.18.cloned.1.call-start = ((), (), s32[]{:S(2)}) async-start(), calls=%async_computation.4 | async-start | bytes 4718592 | tf_op jit(solution)/shard_map/all_gather | solution.py:36
  92.9 64.2 %all-to-all-start.1 = ((f32[16,64,1024]{2,1,0:T(8,128)}), f32[16,64,1024]{2,1,0:T(8,128)}, u32[]{:S(2)}, u32[]{:S(2)}) async-start(f32[16,64,1024]{2,1,0:T(8,128)} %stack.10), calls=%async_computation.1 | async-start | bytes 8388608 | tf_op jit(solution)/shard_map/all_to_all | solution.py:34
  97.4 286.3 %all-gather.16.cloned.1.call-start = ((), (), s32[]{:S(2)}) async-start(), calls=%async_computation.3 | async-start | bytes 4718592 | tf_op jit(solution)/shard_map/all_gather | solution.py:36
  159.6 4.7 %copy-start.2 = (f32[3,128,1024]{2,1,0:T(8,128)S(1)}, f32[3,128,1024]{2,1,0:T(8,128)}, u32[]{:S(2)}) copy-start(f32[3,128,1024]{2,1,0:T(8,128)} %param.9) | copy-start | bytes 4718596
  159.6 112.7 %copy-start.4 = (s32[3,128]{1,0:T(4,128)S(1)}, s32[3,128]{1,0:T(4,128)}, u32[]{:S(2)}) copy-start(s32[3,128]{1,0:T(4,128)} %param.12) | copy-start | bytes 4612
  159.6 112.7 %copy-start.6 = (f32[64]{0:T(128)S(1)}, f32[64]{0:T(128)}, u32[]{:S(2)}) copy-start(f32[64]{0:T(128)} %param.13) | copy-start | bytes 772
  159.6 112.8 %copy-start.5 = (f32[3,128]{1,0:T(4,128)S(1)}, f32[3,128]{1,0:T(4,128)}, u32[]{:S(2)}) copy-start(f32[3,128]{1,0:T(4,128)} %param.11) | copy-start | bytes 4612
  159.6 184.5 %all-to-all-start = ((f32[16,64,1024]{2,1,0:T(8,128)}), f32[16,64,1024]{2,1,0:T(8,128)}, u32[]{:S(2)}, u32[]{:S(2)}) async-start(f32[16,64,1024]{2,1,0:T(8,128)} %stack.9), calls=%async_computation | async-start | bytes 8388608 | tf_op jit(solution)/shard_map/all_to_all | solution.py:34
  383.7 31.8 %copy-start.1 = (f32[1024]{0:T(1024)S(1)}, f32[1024]{0:T(1024)}, u32[]{:S(2)}) copy-start(f32[1024]{0:T(1024)} %param.10) | copy-start | bytes 12292
Sparse Core Ops, SparseCore 0:
  9.7 96.5 all-gather.19
  108.6 86.0 all-gather.17
  197.1 73.6 all-gather.15
